TPU v7x, 512 devices: a whole 4x4x16 slice. The times are simulated.
512 devices in a mesh: gx: 16 (over z_hi, y, core), gy: 32 (over z_lo, x).
Axes of the slice: x: 4, y: 4, z: 16 (z_hi: 2, z_lo: 8; z = z_hi * 8 + z_lo), core: 2. Of those that a mesh axis runs over, the one named last changes fastest.
Arguments:
- adjoint_in: float32 [19, 256, 4, 4096], P(None, 'gx', None, 'gy'), may hold values from -6 to 6
- velocity: bfloat16 [2, 3, 256, 4, 4096], P(None, None, 'gx', None, 'gy')
- solid_tiles: int32 [64, 4, 1024], P('gx', None, 'gy'), may hold values from 0 to 1, as said below
- link_blocked: int32 [18, 256, 4, 4096], P(None, 'gx', None, 'gy'), may hold values from 0 to 1, as said below
Outputs:
- adjoint_out: float32 [19, 256, 4, 4096], P(None, 'gx', None, 'gy')
- drag_sens: float32 [1], replicated
Inputs may be any that keep to these rules, and one draw needn't show every extreme that they name: `solid_tiles`: 1 on the levels below a tile's building height, heights 0 to 3 per tile. `link_blocked`: entry i - 1 is 1 exactly where the cell x + c_i (periodic in the plane) is solid or lies outside the 4 levels.
All inputs are finite; a program needn't handle non-finite values.
Results may differ from a plain program's by a relative error of at most 0.0003.
Values sent between devices are 32-bit elements; how exact they have to be, the bound alone decides.
A program may use at most 64 MiB of HBM per device.

v0:
```python
import math
import jax
import jax.numpy as jnp
from jax import lax
from jax.sharding import PartitionSpec as P

TILE = 4
STEPS = 2
lattice_speeds = (
    (0, 0, 0),
    (1, 0, 0),
    (-1, 0, 0),
    (0, 1, 0),
    (0, -1, 0),
    (0, 0, 1),
    (0, 0, -1),
    (1, 1, 0),
    (-1, -1, 0),
    (1, -1, 0),
    (-1, 1, 0),
    (1, 0, 1),
    (-1, 0, -1),
    (1, 0, -1),
    (-1, 0, 1),
    (0, 1, 1),
    (0, -1, -1),
    (0, 1, -1),
    (0, -1, 1),
)
lattice_weights = (1.0 / 3.0,) + (1.0 / 18.0,) * 6 + (1.0 / 36.0,) * 12
relax_rate = 1.6
drag_factor = 20.0


def with_halo(block, sides, width):
    for axis, dim in sides:
        count = lax.axis_size(axis)
        forward = [(i, i + 1) for i in range(count - 1)]
        forward.append((count - 1, 0))
        backward = [(target, source) for source, target in forward]
        low = lax.ppermute(
            lax.slice_in_dim(block, block.shape[dim] - width, None, axis=dim), axis, forward
        )
        high = lax.ppermute(lax.slice_in_dim(block, 0, width, axis=dim), axis, backward)
        block = jnp.concatenate([low, block, high], axis=dim)
    return block


def opposite_of(number):
    return number + 1 if number % 2 == 1 else number - 1


def shift_level(field, lift):
    if lift == 1:
        return jnp.concatenate([field[:, 1:], jnp.zeros_like(field[:, :1])], axis=1)
    if lift == -1:
        return jnp.concatenate([jnp.zeros_like(field[:, :1]), field[:, :-1]], axis=1)
    return field


def adjoint_collide(moved, flow, fluid):
    speed_sq = flow[0] * flow[0] + flow[1] * flow[1] + flow[2] * flow[2]
    scalar_part = jnp.zeros_like(speed_sq)
    vector_part = [jnp.zeros_like(speed_sq) for axis_number in range(3)]
    drag_local = jnp.zeros_like(speed_sq)
    for number in range(19):
        speed = lattice_speeds[number]
        along = speed[0] * flow[0] + speed[1] * flow[1] + speed[2] * flow[2]
        weighted = lattice_weights[number] * moved[number]
        scalar_part = scalar_part + weighted * (
            1.0 + 3.0 * along + 4.5 * along * along - 1.5 * speed_sq
        )
        for axis_number in range(3):
            vector_part[axis_number] = vector_part[axis_number] + weighted * (
                3.0 * speed[axis_number]
                + 9.0 * along * speed[axis_number]
                - 3.0 * flow[axis_number]
            )
        drag_local = drag_local + 3.0 * weighted * along
    results = []
    for number in range(19):
        speed = lattice_speeds[number]
        projected = scalar_part
        for axis_number in range(3):
            projected = projected + vector_part[axis_number] * (
                speed[axis_number] - flow[axis_number]
            )
        results.append(fluid * ((1.0 - relax_rate) * moved[number] + relax_rate * projected))
    return (jnp.stack(results), fluid * drag_local)


def stream_back(padded, centre, blocked, span_x, span_y):
    moved = [centre[0]]
    for number in range(1, 19):
        speed = lattice_speeds[number]
        source = padded[
            number, 1 + speed[0] : 1 + speed[0] + span_x, :, 1 + speed[1] : 1 + speed[1] + span_y
        ]
        source = shift_level(source, speed[2])
        bounced = centre[opposite_of(number)] + 2.0 * speed[0]
        moved.append(jnp.where(blocked[number - 1] == 1, bounced, source))
    return moved


def per_device(adjoint_in, velocity, solid_tiles, link_blocked):
    rows_x = adjoint_in.shape[1]
    rows_y = adjoint_in.shape[3]
    levels = adjoint_in.shape[2]
    solid = jnp.repeat(jnp.repeat(solid_tiles, TILE, axis=0), TILE, axis=2)
    fluid = 1.0 - solid.astype(jnp.float32)
    state = adjoint_in
    step_terms = []
    for adjoint_step in range(STEPS):
        flow = velocity[adjoint_step].astype(jnp.float32)
        padded = with_halo(state, (("gx", 1), ("gy", 3)), 1)
        moved = stream_back(padded, state, link_blocked, rows_x, rows_y)
        state, drag_field = adjoint_collide(moved, flow, fluid)
        step_terms.append(jnp.sum(drag_field))
    total = jnp.zeros((), jnp.float32)
    for adjoint_step in range(STEPS):
        total = total + lax.psum(step_terms[adjoint_step], ("gx", "gy"))
    cell_count = rows_x * lax.axis_size("gx") * rows_y * lax.axis_size("gy") * levels
    scale = drag_factor / math.sqrt(cell_count)
    return (state, (-scale * total).reshape(1))


def solution(mesh):
    placed = (
        P(None, "gx", None, "gy"),
        P(None, None, "gx", None, "gy"),
        P("gx", None, "gy"),
        P(None, "gx", None, "gy"),
    )
    return jax.shard_map(
        per_device,
        mesh=mesh,
        in_specs=placed,
        out_specs=(P(None, "gx", None, "gy"), P()),
        check_vma=False,
    )
```

profile of v0, /device:TPU:1, one launch (start us, length us, event | category | flops | bytes accessed | tf_op | source)
XLA Modules:
  0.0 222.9 jit_solution(16425646416944457608)
XLA Ops:
  0.6 0.8 fusion.265
  1.4 4.6 %collective-permute-start.1 = (f32[19,1,4,128]{3,2,1,0:T(4,128)S(1)}, f32[19,1,4,128]{3,2,1,0:T(4,128)S(1)}, u32[]{:S(2)}, u32[]{:S(2)}) collective-permute-start(f32[19,1,4,128]{3,2,1,0:T(4,128)S(1)} %get-tuple-element.193), channel_id=1, source_target_pairs={{0,32},{32,64},{64,96},{96,128},{128,160},{160,192},{192,224},{224... | collective-permute-start | bytes 116744 | tf_op jit(solution)/shard_map/ppermute | solution.py:41
  6.0 6.2 %collective-permute-start = (f32[19,1,4,128]{3,2,1,0:T(4,128)S(1)}, f32[19,1,4,128]{3,2,1,0:T(4,128)S(1)}, u32[]{:S(2)}, u32[]{:S(2)}) collective-permute-start(f32[19,1,4,128]{3,2,1,0:T(4,128)S(1)} %get-tuple-element.194), channel_id=1, source_target_pairs={{32,0},{64,32},{96,64},{128,96},{160,128},{192,160},{224,192},{256... | collective-permute-start | bytes 116744 | tf_op jit(solution)/shard_map/ppermute | solution.py:44
  12.3 1.7 fusion.264
  14.1 0.8 fusion.266
  15.0 0.6 copy-done.67
  15.9 0.6 slice.360
  16.5 0.6 slice.361
  17.6 0.6 fusion.262
  18.3 0.6 fusion.261
  20.4 10.9 %collective-permute-start.2 = (f32[19,18,4,1]{0,2,3,1:T(4,128)S(1)}, f32[19,18,4,1]{0,2,3,1:T(4,128)}, u32[]{:S(2)}, u32[]{:S(2)}) collective-permute-start(f32[19,18,4,1]{0,2,3,1:T(4,128)S(1)} %copy.538), channel_id=1, source_target_pairs={{1,0},{2,1},{3,2},{4,3},{5,4},{6,5},{7,6},{8,7},{9,8},{10,9},{11,1... | collective-permute-start | bytes 16424 | tf_op jit(solution)/shard_map/ppermute | solution.py:44
  31.3 1.9 collective-permute-start.3
  33.3 0.6 slice.367
  33.9 0.6 slice.363
  34.5 0.6 slice.369
  35.2 0.6 slice.365
  35.8 8.9 %collective-permute-done.3 = f32[19,18,4,1]{0,2,3,1:T(4,128)S(1)} collective-permute-done((f32[19,18,4,1]{0,2,3,1:T(4,128)S(1)}, f32[19,18,4,1]{0,2,3,1:T(4,128)S(1)}, u32[]{:S(2)}, u32[]{:S(2)}) %collective-permute-start.3) | collective-permute-done | bytes 5504 | tf_op jit(solution)/shard_map/ppermute | solution.py:41
  44.7 1.0 copy.442
  45.7 1.8 copy.438
  48.9 1.7 multiply_reduce_fusion.1
  51.4 0.6 constant_dynamic-update-slice_fusion.17
  52.0 0.6 constant_dynamic-update-slice_fusion.16
  52.6 0.6 constant_dynamic-update-slice_fusion.15
  53.2 0.6 constant_dynamic-update-slice_fusion.14
  53.9 0.6 constant_dynamic-update-slice_fusion.13
  54.5 0.6 constant_dynamic-update-slice_fusion.12
  55.1 0.6 constant_dynamic-update-slice_fusion.11
  55.8 0.6 constant_dynamic-update-slice_fusion.10
  56.4 0.6 constant_dynamic-update-slice_fusion.9
  57.0 0.6 constant_dynamic-update-slice_fusion.8
  57.6 0.6 constant_dynamic-update-slice_fusion.7
  58.3 14.7 %collective-permute-start.4 = (f32[19,1,4,128]{3,2,1,0:T(4,128)S(1)}, f32[19,1,4,128]{3,2,1,0:T(4,128)S(1)}, u32[]{:S(2)}, u32[]{:S(2)}) collective-permute-start(f32[19,1,4,128]{3,2,1,0:T(4,128)S(1)} %bitcast.557), channel_id=1, source_target_pairs={{32,0},{64,32},{96,64},{128,96},{160,128},{192,160},{224,192},{256... | collective-permute-start | bytes 116744 | tf_op jit(solution)/shard_map/ppermute | solution.py:44
  73.0 1.9 collective-permute-start.5
  75.0 0.6 slice.382
  75.6 0.6 slice.381
  76.2 6.9 %collective-permute-done.5 = f32[19,1,4,128]{3,2,1,0:T(4,128)S(1)} collective-permute-done((f32[19,1,4,128]{3,2,1,0:T(4,128)S(1)}, f32[19,1,4,128]{3,2,1,0:T(4,128)S(1)}, u32[]{:S(2)}, u32[]{:S(2)}) %collective-permute-start.5) | collective-permute-done | bytes 38944 | tf_op jit(solution)/shard_map/ppermute | solution.py:41
  83.6 0.6 copy.504
  84.8 3.1 %collective-permute-start.6 = (f32[19,18,4,1]{0,2,3,1:T(4,128)S(1)}, f32[19,18,4,1]{0,2,3,1:T(4,128)S(1)}, u32[]{:S(2)}, u32[]{:S(2)}) collective-permute-start(f32[19,18,4,1]{0,2,3,1:T(4,128)S(1)} %copy.502), channel_id=1, source_target_pairs={{1,0},{2,1},{3,2},{4,3},{5,4},{6,5},{7,6},{8,7},{9,8},{10,9},{11,1... | collective-permute-start | bytes 16424 | tf_op jit(solution)/shard_map/ppermute | solution.py:44
  87.9 2.1 collective-permute-start.7
  90.1 0.6 slice.385
  90.7 0.6 slice.383
  91.3 0.6 slice.386
  91.9 9.4 %collective-permute-done.7 = f32[19,18,4,1]{0,2,3,1:T(4,128)S(1)} collective-permute-done((f32[19,18,4,1]{0,2,3,1:T(4,128)S(1)}, f32[19,18,4,1]{0,2,3,1:T(4,128)S(1)}, u32[]{:S(2)}, u32[]{:S(2)}) %collective-permute-start.7) | collective-permute-done | bytes 5504 | tf_op jit(solution)/shard_map/ppermute | solution.py:41
  101.3 1.0 copy.505
  102.4 1.1 copy.503
  104.8 1.6 multiply_reduce_fusion
  107.7 111.4 %psum.16 = f32[]{:T(128)} all-reduce(f32[]{:T(128)S(6)} %add.2107), channel_id=1, replica_groups=mesh['gx'=16,'gy'=32] {'gx','gy'}, use_global_device_ids=true, to_apply=%region_1.2 | all-reduce | flops 1 | bytes 8 | tf_op jit(solution)/shard_map/psum | solution.py:121
  220.1 1.1 copy.527
  (201 shorter events, 7.3 us)
Async XLA Ops:
  1.4 15.7 %collective-permute-start.1 = (f32[19,1,4,128]{3,2,1,0:T(4,128)S(1)}, f32[19,1,4,128]{3,2,1,0:T(4,128)S(1)}, u32[]{:S(2)}, u32[]{:S(2)}) collective-permute-start(f32[19,1,4,128]{3,2,1,0:T(4,128)S(1)} %get-tuple-element.193), channel_id=1, source_target_pairs={{0,32},{32,64},{64,96},{96,128},{128,160},{160,192},{192,224},{224... | collective-permute-start | bytes 116744 | tf_op jit(solution)/shard_map/ppermute | solution.py:41
  6.0 8.0 %copy-start.48 = (bf16[2,3,16,4,128]{4,3,2,1,0:T(4,128)(2,1)S(1)}, bf16[2,3,16,4,128]{4,3,2,1,0:T(4,128)(2,1)}, u32[]{:S(2)}) copy-start(bf16[2,3,16,4,128]{4,3,2,1,0:T(4,128)(2,1)} %param.5) | copy-start | bytes 294916
  6.0 8.1 %copy-start.1 = (s32[18,16,4,128]{3,2,1,0:T(4,128)S(1)}, s32[18,16,4,128]{3,2,1,0:T(4,128)}, u32[]{:S(2)}) copy-start(s32[18,16,4,128]{3,2,1,0:T(4,128)} %param.7) | copy-start | bytes 1769476
  6.0 11.5 %collective-permute-start = (f32[19,1,4,128]{3,2,1,0:T(4,128)S(1)}, f32[19,1,4,128]{3,2,1,0:T(4,128)S(1)}, u32[]{:S(2)}, u32[]{:S(2)}) collective-permute-start(f32[19,1,4,128]{3,2,1,0:T(4,128)S(1)} %get-tuple-element.194), channel_id=1, source_target_pairs={{32,0},{64,32},{96,64},{128,96},{160,128},{192,160},{224,192},{256... | collective-permute-start | bytes 116744 | tf_op jit(solution)/shard_map/ppermute | solution.py:44
  15.0 2.2 copy-start
  20.4 25.3 %collective-permute-start.2 = (f32[19,18,4,1]{0,2,3,1:T(4,128)S(1)}, f32[19,18,4,1]{0,2,3,1:T(4,128)}, u32[]{:S(2)}, u32[]{:S(2)}) collective-permute-start(f32[19,18,4,1]{0,2,3,1:T(4,128)S(1)} %copy.538), channel_id=1, source_target_pairs={{1,0},{2,1},{3,2},{4,3},{5,4},{6,5},{7,6},{8,7},{9,8},{10,9},{11,1... | collective-permute-start | bytes 16424 | tf_op jit(solution)/shard_map/ppermute | solution.py:44
  31.3 13.4 %collective-permute-start.3 = (f32[19,18,4,1]{0,2,3,1:T(4,128)S(1)}, f32[19,18,4,1]{0,2,3,1:T(4,128)S(1)}, u32[]{:S(2)}, u32[]{:S(2)}) collective-permute-start(f32[19,18,4,1]{0,2,3,1:T(4,128)S(1)} %copy.541), channel_id=1, source_target_pairs={{0,1},{1,2},{2,3},{3,4},{4,5},{5,6},{6,7},{7,8},{8,9},{9,10},{10,1... | collective-permute-start | bytes 16424 | tf_op jit(solution)/shard_map/ppermute | solution.py:41
  47.6 0.8 copy-start.15
  47.6 0.8 copy-start.16
  47.6 0.8 copy-start.17
  47.6 0.8 copy-start.18
  47.7 0.8 copy-start.19
  47.7 0.8 copy-start.20
  47.7 0.9 copy-start.21
  47.7 0.9 copy-start.22
  47.7 0.9 copy-start.23
  47.7 0.9 copy-start.35
  47.7 0.9 copy-start.36
  47.7 0.9 copy-start.37
  47.7 0.9 copy-start.38
  47.7 0.9 copy-start.41
  47.8 0.9 copy-start.42
  47.8 0.9 copy-start.43
  47.8 0.9 copy-start.45
  47.9 0.8 copy-start.9
  47.9 0.8 copy-start.10
  47.9 0.8 copy-start.8
  48.0 0.8 copy-start.6
  48.0 0.8 copy-start.7
  48.0 0.8 copy-start.4
  48.0 0.8 copy-start.2
  48.0 0.8 copy-start.3
  58.3 17.9 %collective-permute-start.4 = (f32[19,1,4,128]{3,2,1,0:T(4,128)S(1)}, f32[19,1,4,128]{3,2,1,0:T(4,128)S(1)}, u32[]{:S(2)}, u32[]{:S(2)}) collective-permute-start(f32[19,1,4,128]{3,2,1,0:T(4,128)S(1)} %bitcast.557), channel_id=1, source_target_pairs={{32,0},{64,32},{96,64},{128,96},{160,128},{192,160},{224,192},{256... | collective-permute-start | bytes 116744 | tf_op jit(solution)/shard_map/ppermute | solution.py:44
  73.0 10.1 %collective-permute-start.5 = (f32[19,1,4,128]{3,2,1,0:T(4,128)S(1)}, f32[19,1,4,128]{3,2,1,0:T(4,128)S(1)}, u32[]{:S(2)}, u32[]{:S(2)}) collective-permute-start(f32[19,1,4,128]{3,2,1,0:T(4,128)S(1)} %bitcast.556), channel_id=1, source_target_pairs={{0,32},{32,64},{64,96},{96,128},{128,160},{160,192},{192,224},{224... | collective-permute-start | bytes 116744 | tf_op jit(solution)/shard_map/ppermute | solution.py:41
  84.8 17.6 %collective-permute-start.6 = (f32[19,18,4,1]{0,2,3,1:T(4,128)S(1)}, f32[19,18,4,1]{0,2,3,1:T(4,128)S(1)}, u32[]{:S(2)}, u32[]{:S(2)}) collective-permute-start(f32[19,18,4,1]{0,2,3,1:T(4,128)S(1)} %copy.502), channel_id=1, source_target_pairs={{1,0},{2,1},{3,2},{4,3},{5,4},{6,5},{7,6},{8,7},{9,8},{10,9},{11,1... | collective-permute-start | bytes 16424 | tf_op jit(solution)/shard_map/ppermute | solution.py:44
  87.9 13.4 %collective-permute-start.7 = (f32[19,18,4,1]{0,2,3,1:T(4,128)S(1)}, f32[19,18,4,1]{0,2,3,1:T(4,128)S(1)}, u32[]{:S(2)}, u32[]{:S(2)}) collective-permute-start(f32[19,18,4,1]{0,2,3,1:T(4,128)S(1)} %copy.504), channel_id=1, source_target_pairs={{0,1},{1,2},{2,3},{3,4},{4,5},{5,6},{6,7},{7,8},{8,9},{9,10},{10,1... | collective-permute-start | bytes 16424 | tf_op jit(solution)/shard_map/ppermute | solution.py:41
  103.6 0.8 copy-start.55
  103.6 0.8 copy-start.56
  103.6 0.8 copy-start.57
  103.6 0.8 copy-start.58
  103.6 0.8 copy-start.59
  103.6 0.8 copy-start.60
  103.6 0.8 copy-start.61
  103.6 0.8 copy-start.62
  103.6 0.8 copy-start.63
  104.0 0.8 copy-start.5
  104.0 0.8 copy-start.24
  106.4 112.7 %copy-start.34 = (f32[16,4,128]{2,0,1:T(8,128)S(1)}, f32[16,4,128]{2,0,1:T(8,128)}, u32[]{:S(2)}) copy-start(f32[16,4,128]{2,0,1:T(8,128)} %get-tuple-element.15) | copy-start | bytes 98308
  (28 other events, 21.9 us)
where the time goes:
time: 224 us; the launch traced here: 223 us
  blocking collectives  111 us (50%)
  starting transfers between devices  45.5 us (20%)
  waiting for transfers between devices  25.3 us (11%)
  local copies, waits for them, and re-layouts  23.7 us (11%)
  other arithmetic  12.3 us (5%)
  between operations  4.66 us (2%)
    psum x1, blocking collectives, per_device(): total = total + lax.psum(step_terms[adjoint_step], ('gx', 'gy'))  111 us
    ppermute x4, starting transfers between devices, with_halo(): lax.ppermute(lax.slice_in_dim(block, 0, width, axis=dim), axis, backward)  35 us
    ppermute x4, waiting for transfers between devices, with_halo(): lax.ppermute(lax.slice_in_dim(block, block.shape[dim] - width, None, axis...  25.3 us
    ppermute x4, starting transfers between devices, with_halo(): lax.ppermute(lax.slice_in_dim(block, block.shape[dim] - width, None, axis...  10.6 us
    unnamed x36, other arithmetic  7.93 us
    unnamed x141, local copies, waits for them, and re-layouts  5 us
  transfers between devices with their start and end apart: 8, of which 3 were waited for; matrix products, arithmetic and copies ran while one was open for 5% of the time, Pallas kernels for 0%

commit v1 on v0

--- a/solution.py
+++ b/solution.py
@@ -118,7 +118,7 @@
         step_terms.append(jnp.sum(drag_field))
     total = jnp.zeros((), jnp.float32)
     for adjoint_step in range(STEPS):
-        total = total + lax.psum(step_terms[adjoint_step], ("gx", "gy"))
+        total = total + lax.psum(lax.psum(step_terms[adjoint_step], "gy"), "gx")
     cell_count = rows_x * lax.axis_size("gx") * rows_y * lax.axis_size("gy") * levels
     scale = drag_factor / math.sqrt(cell_count)
     return (state, (-scale * total).reshape(1))

time: 224 us -> 302 us (1.35)
  blocking collectives: 111 us -> 190 us
    psum x1 -> x2, blocking collectives: 111 us -> 190 us  [per_device(): total = total + lax.psum(lax.psum(step_terms[adjoint_step], 'gy'), 'gx')]
  transfers between devices with their start and end apart: 8 -> 8, of which waited for: 3 -> 3; matrix products, arithmetic and copies ran while one was open for 5% -> 4% of each run, Pallas kernels for 0% -> 0%
where the time goes in v1:
time: 302 us
  blocking collectives  190 us (63%)
  starting transfers between devices  45.5 us (15%)
  waiting for transfers between devices  25.3 us (8%)
  local copies, waits for them, and re-layouts  23.6 us (8%)
  other arithmetic  12.2 us (4%)
  between operations  4.61 us (2%)
    psum x2, blocking collectives, per_device(): total = total + lax.psum(lax.psum(step_terms[adjoint_step], 'gy'), 'gx')  190 us
    ppermute x4, starting transfers between devices, with_halo(): lax.ppermute(lax.slice_in_dim(block, 0, width, axis=dim), axis, backward)  35 us
    ppermute x4, waiting for transfers between devices, with_halo(): lax.ppermute(lax.slice_in_dim(block, block.shape[dim] - width, None, axis...  25.3 us
    ppermute x4, starting transfers between devices, with_halo(): lax.ppermute(lax.slice_in_dim(block, block.shape[dim] - width, None, axis...  10.6 us
    unnamed x36, other arithmetic  7.84 us
  transfers between devices with their start and end apart: 8, of which 3 were waited for; matrix products, arithmetic and copies ran while one was open for 4% of the time, Pallas kernels for 0%

profile of v1, /device:TPU:1, one launch (start us, length us, event | category | flops | bytes accessed | tf_op | source)
XLA Modules:
  0.0 301.5 jit_solution(12882433771769041623)
XLA Ops:
  0.6 0.8 fusion.265
  1.4 4.6 %collective-permute-start.1 = (f32[19,1,4,128]{3,2,1,0:T(4,128)S(1)}, f32[19,1,4,128]{3,2,1,0:T(4,128)S(1)}, u32[]{:S(2)}, u32[]{:S(2)}) collective-permute-start(f32[19,1,4,128]{3,2,1,0:T(4,128)S(1)} %get-tuple-element.193), channel_id=1, source_target_pairs={{0,32},{32,64},{64,96},{96,128},{128,160},{160,192},{192,224},{224... | collective-permute-start | bytes 116744 | tf_op jit(solution)/shard_map/ppermute | solution.py:41
  6.0 6.2 %collective-permute-start = (f32[19,1,4,128]{3,2,1,0:T(4,128)S(1)}, f32[19,1,4,128]{3,2,1,0:T(4,128)S(1)}, u32[]{:S(2)}, u32[]{:S(2)}) collective-permute-start(f32[19,1,4,128]{3,2,1,0:T(4,128)S(1)} %get-tuple-element.194), channel_id=1, source_target_pairs={{32,0},{64,32},{96,64},{128,96},{160,128},{192,160},{224,192},{256... | collective-permute-start | bytes 116744 | tf_op jit(solution)/shard_map/ppermute | solution.py:44
  12.3 1.7 fusion.264
  14.1 0.8 fusion.266
  15.0 0.6 copy-done.67
  15.9 0.6 slice.360
  16.5 0.6 slice.361
  17.6 0.6 fusion.262
  18.2 0.6 fusion.261
  20.3 10.9 %collective-permute-start.2 = (f32[19,18,4,1]{0,2,3,1:T(4,128)S(1)}, f32[19,18,4,1]{0,2,3,1:T(4,128)}, u32[]{:S(2)}, u32[]{:S(2)}) collective-permute-start(f32[19,18,4,1]{0,2,3,1:T(4,128)S(1)} %copy.538), channel_id=1, source_target_pairs={{1,0},{2,1},{3,2},{4,3},{5,4},{6,5},{7,6},{8,7},{9,8},{10,9},{11,1... | collective-permute-start | bytes 16424 | tf_op jit(solution)/shard_map/ppermute | solution.py:44
  31.2 1.9 collective-permute-start.3
  33.3 0.6 slice.367
  33.9 0.6 slice.363
  34.5 0.6 slice.369
  35.1 0.6 slice.365
  35.7 8.9 %collective-permute-done.3 = f32[19,18,4,1]{0,2,3,1:T(4,128)S(1)} collective-permute-done((f32[19,18,4,1]{0,2,3,1:T(4,128)S(1)}, f32[19,18,4,1]{0,2,3,1:T(4,128)S(1)}, u32[]{:S(2)}, u32[]{:S(2)}) %collective-permute-start.3) | collective-permute-done | bytes 5504 | tf_op jit(solution)/shard_map/ppermute | solution.py:41
  44.7 1.0 copy.442
  45.7 1.8 copy.438
  48.8 1.7 multiply_reduce_fusion.1
  51.3 0.6 constant_dynamic-update-slice_fusion.17
  52.0 0.6 constant_dynamic-update-slice_fusion.16
  52.6 0.6 constant_dynamic-update-slice_fusion.15
  53.2 0.6 constant_dynamic-update-slice_fusion.14
  53.8 0.6 constant_dynamic-update-slice_fusion.13
  54.4 0.6 constant_dynamic-update-slice_fusion.12
  55.0 0.6 constant_dynamic-update-slice_fusion.11
  55.7 0.6 constant_dynamic-update-slice_fusion.10
  56.3 0.6 constant_dynamic-update-slice_fusion.9
  56.9 0.6 constant_dynamic-update-slice_fusion.8
  57.5 0.6 constant_dynamic-update-slice_fusion.7
  58.2 14.7 %collective-permute-start.4 = (f32[19,1,4,128]{3,2,1,0:T(4,128)S(1)}, f32[19,1,4,128]{3,2,1,0:T(4,128)S(1)}, u32[]{:S(2)}, u32[]{:S(2)}) collective-permute-start(f32[19,1,4,128]{3,2,1,0:T(4,128)S(1)} %bitcast.557), channel_id=1, source_target_pairs={{32,0},{64,32},{96,64},{128,96},{160,128},{192,160},{224,192},{256... | collective-permute-start | bytes 116744 | tf_op jit(solution)/shard_map/ppermute | solution.py:44
  72.9 1.9 collective-permute-start.5
  74.8 0.6 slice.382
  75.4 0.6 slice.381
  76.0 7.0 %collective-permute-done.5 = f32[19,1,4,128]{3,2,1,0:T(4,128)S(1)} collective-permute-done((f32[19,1,4,128]{3,2,1,0:T(4,128)S(1)}, f32[19,1,4,128]{3,2,1,0:T(4,128)S(1)}, u32[]{:S(2)}, u32[]{:S(2)}) %collective-permute-start.5) | collective-permute-done | bytes 38944 | tf_op jit(solution)/shard_map/ppermute | solution.py:41
  84.7 3.1 %collective-permute-start.6 = (f32[19,18,4,1]{0,2,3,1:T(4,128)S(1)}, f32[19,18,4,1]{0,2,3,1:T(4,128)S(1)}, u32[]{:S(2)}, u32[]{:S(2)}) collective-permute-start(f32[19,18,4,1]{0,2,3,1:T(4,128)S(1)} %copy.502), channel_id=1, source_target_pairs={{1,0},{2,1},{3,2},{4,3},{5,4},{6,5},{7,6},{8,7},{9,8},{10,9},{11,1... | collective-permute-start | bytes 16424 | tf_op jit(solution)/shard_map/ppermute | solution.py:44
  87.8 2.1 collective-permute-start.7
  90.0 0.6 slice.385
  90.6 0.6 slice.383
  91.2 0.6 slice.386
  91.8 9.4 %collective-permute-done.7 = f32[19,18,4,1]{0,2,3,1:T(4,128)S(1)} collective-permute-done((f32[19,18,4,1]{0,2,3,1:T(4,128)S(1)}, f32[19,18,4,1]{0,2,3,1:T(4,128)S(1)}, u32[]{:S(2)}, u32[]{:S(2)}) %collective-permute-start.7) | collective-permute-done | bytes 5504 | tf_op jit(solution)/shard_map/ppermute | solution.py:41
  101.2 1.0 copy.505
  102.3 1.1 copy.503
  104.7 1.6 multiply_reduce_fusion
  107.5 100.0 %psum.33 = f32[]{:T(128)} all-reduce(f32[]{:T(128)S(6)} %add.2111), channel_id=1, replica_groups=mesh['gx'=16,'gy'=32] {'gy'}, use_global_device_ids=true, to_apply=%region_1.2 | all-reduce | flops 1 | bytes 8 | tf_op jit(solution)/shard_map/psum | solution.py:121
  207.5 90.2 %psum.32 = f32[]{:T(128)} all-reduce(f32[]{:T(128)} %psum.33), channel_id=1, replica_groups=mesh['gx'=16,'gy'=32] {'gx'}, use_global_device_ids=true, to_apply=%region_2.3 | all-reduce | flops 1 | bytes 8 | tf_op jit(solution)/shard_map/psum | solution.py:121
  298.7 1.1 copy.527
  (202 shorter events, 7.9 us)
Async XLA Ops:
  1.4 15.7 %collective-permute-start.1 = (f32[19,1,4,128]{3,2,1,0:T(4,128)S(1)}, f32[19,1,4,128]{3,2,1,0:T(4,128)S(1)}, u32[]{:S(2)}, u32[]{:S(2)}) collective-permute-start(f32[19,1,4,128]{3,2,1,0:T(4,128)S(1)} %get-tuple-element.193), channel_id=1, source_target_pairs={{0,32},{32,64},{64,96},{96,128},{128,160},{160,192},{192,224},{224... | collective-permute-start | bytes 116744 | tf_op jit(solution)/shard_map/ppermute | solution.py:41
  6.0 8.0 %copy-start.48 = (bf16[2,3,16,4,128]{4,3,2,1,0:T(4,128)(2,1)S(1)}, bf16[2,3,16,4,128]{4,3,2,1,0:T(4,128)(2,1)}, u32[]{:S(2)}) copy-start(bf16[2,3,16,4,128]{4,3,2,1,0:T(4,128)(2,1)} %param.5) | copy-start | bytes 294916
  6.0 8.0 %copy-start.1 = (s32[18,16,4,128]{3,2,1,0:T(4,128)S(1)}, s32[18,16,4,128]{3,2,1,0:T(4,128)}, u32[]{:S(2)}) copy-start(s32[18,16,4,128]{3,2,1,0:T(4,128)} %param.7) | copy-start | bytes 1769476
  6.0 11.5 %collective-permute-start = (f32[19,1,4,128]{3,2,1,0:T(4,128)S(1)}, f32[19,1,4,128]{3,2,1,0:T(4,128)S(1)}, u32[]{:S(2)}, u32[]{:S(2)}) collective-permute-start(f32[19,1,4,128]{3,2,1,0:T(4,128)S(1)} %get-tuple-element.194), channel_id=1, source_target_pairs={{32,0},{64,32},{96,64},{128,96},{160,128},{192,160},{224,192},{256... | collective-permute-start | bytes 116744 | tf_op jit(solution)/shard_map/ppermute | solution.py:44
  14.9 2.2 copy-start
  20.3 25.3 %collective-permute-start.2 = (f32[19,18,4,1]{0,2,3,1:T(4,128)S(1)}, f32[19,18,4,1]{0,2,3,1:T(4,128)}, u32[]{:S(2)}, u32[]{:S(2)}) collective-permute-start(f32[19,18,4,1]{0,2,3,1:T(4,128)S(1)} %copy.538), channel_id=1, source_target_pairs={{1,0},{2,1},{3,2},{4,3},{5,4},{6,5},{7,6},{8,7},{9,8},{10,9},{11,1... | collective-permute-start | bytes 16424 | tf_op jit(solution)/shard_map/ppermute | solution.py:44
  31.2 13.4 %collective-permute-start.3 = (f32[19,18,4,1]{0,2,3,1:T(4,128)S(1)}, f32[19,18,4,1]{0,2,3,1:T(4,128)S(1)}, u32[]{:S(2)}, u32[]{:S(2)}) collective-permute-start(f32[19,18,4,1]{0,2,3,1:T(4,128)S(1)} %copy.541), channel_id=1, source_target_pairs={{0,1},{1,2},{2,3},{3,4},{4,5},{5,6},{6,7},{7,8},{8,9},{9,10},{10,1... | collective-permute-start | bytes 16424 | tf_op jit(solution)/shard_map/ppermute | solution.py:41
  47.6 0.8 copy-start.15
  47.6 0.8 copy-start.16
  47.6 0.8 copy-start.17
  47.6 0.8 copy-start.18
  47.6 0.8 copy-start.19
  47.6 0.8 copy-start.20
  47.6 0.9 copy-start.21
  47.6 0.9 copy-start.22
  47.6 0.9 copy-start.23
  47.7 0.9 copy-start.35
  47.7 0.9 copy-start.36
  47.7 0.9 copy-start.37
  47.7 0.9 copy-start.38
  47.7 0.9 copy-start.41
  47.7 0.9 copy-start.42
  47.7 0.9 copy-start.43
  47.7 0.9 copy-start.45
  47.9 0.8 copy-start.9
  47.9 0.8 copy-start.10
  47.9 0.8 copy-start.8
  47.9 0.8 copy-start.6
  47.9 0.8 copy-start.7
  47.9 0.8 copy-start.4
  48.0 0.8 copy-start.2
  48.0 0.8 copy-start.3
  58.2 17.9 %collective-permute-start.4 = (f32[19,1,4,128]{3,2,1,0:T(4,128)S(1)}, f32[19,1,4,128]{3,2,1,0:T(4,128)S(1)}, u32[]{:S(2)}, u32[]{:S(2)}) collective-permute-start(f32[19,1,4,128]{3,2,1,0:T(4,128)S(1)} %bitcast.557), channel_id=1, source_target_pairs={{32,0},{64,32},{96,64},{128,96},{160,128},{192,160},{224,192},{256... | collective-permute-start | bytes 116744 | tf_op jit(solution)/shard_map/ppermute | solution.py:44
  72.9 10.1 %collective-permute-start.5 = (f32[19,1,4,128]{3,2,1,0:T(4,128)S(1)}, f32[19,1,4,128]{3,2,1,0:T(4,128)S(1)}, u32[]{:S(2)}, u32[]{:S(2)}) collective-permute-start(f32[19,1,4,128]{3,2,1,0:T(4,128)S(1)} %bitcast.556), channel_id=1, source_target_pairs={{0,32},{32,64},{64,96},{96,128},{128,160},{160,192},{192,224},{224... | collective-permute-start | bytes 116744 | tf_op jit(solution)/shard_map/ppermute | solution.py:41
  84.7 17.6 %collective-permute-start.6 = (f32[19,18,4,1]{0,2,3,1:T(4,128)S(1)}, f32[19,18,4,1]{0,2,3,1:T(4,128)S(1)}, u32[]{:S(2)}, u32[]{:S(2)}) collective-permute-start(f32[19,18,4,1]{0,2,3,1:T(4,128)S(1)} %copy.502), channel_id=1, source_target_pairs={{1,0},{2,1},{3,2},{4,3},{5,4},{6,5},{7,6},{8,7},{9,8},{10,9},{11,1... | collective-permute-start | bytes 16424 | tf_op jit(solution)/shard_map/ppermute | solution.py:44
  87.8 13.4 %collective-permute-start.7 = (f32[19,18,4,1]{0,2,3,1:T(4,128)S(1)}, f32[19,18,4,1]{0,2,3,1:T(4,128)S(1)}, u32[]{:S(2)}, u32[]{:S(2)}) collective-permute-start(f32[19,18,4,1]{0,2,3,1:T(4,128)S(1)} %copy.504), channel_id=1, source_target_pairs={{0,1},{1,2},{2,3},{3,4},{4,5},{5,6},{6,7},{7,8},{8,9},{9,10},{10,1... | collective-permute-start | bytes 16424 | tf_op jit(solution)/shard_map/ppermute | solution.py:41
  103.4 0.8 copy-start.55
  103.4 0.8 copy-start.56
  103.5 0.8 copy-start.57
  103.5 0.8 copy-start.58
  103.5 0.8 copy-start.59
  103.5 0.8 copy-start.60
  103.5 0.8 copy-start.61
  103.5 0.8 copy-start.62
  103.5 0.8 copy-start.63
  103.8 0.8 copy-start.5
  103.8 0.8 copy-start.24
  106.2 191.4 %copy-start.34 = (f32[16,4,128]{2,0,1:T(8,128)S(1)}, f32[16,4,128]{2,0,1:T(8,128)}, u32[]{:S(2)}) copy-start(f32[16,4,128]{2,0,1:T(8,128)} %get-tuple-element.15) | copy-start | bytes 98308
  (28 other events, 21.9 us)
